TPU v7x, 128 devices: a whole 4x4x4 slice. The times are simulated.
128 devices in a mesh: row: 8 (over y, core), col: 16 (over x, z).
Axes of the slice: x: 4, y: 4, z: 4, core: 2. Of those that a mesh axis runs over, the one named last changes fastest.
Arguments:
- theta: float32 [64, 256, 256], P('row', None, 'col'), may hold values from -6 to 6
- left_env: float32 [32, 32, 256, 256], P('row', 'col'), as said below
- right_env: float32 [8, 32, 256, 256], P(None, 'col'), as said below
- left_sector: int32 [64], replicated, may hold values from 0 to 31, as said below
- right_sector: int32 [64], P('row'), may hold values from 0 to 7
- term_on: int32 [64, 32], P('row', 'col'), may hold values 0 or 1
- left_size: int32 [32], replicated, may hold values from 1 to 256, 5120 in all
- right_size: int32 [8], replicated, may hold values from 1 to 256, 1280 in all
Outputs:
- new_theta: float32 [64, 256, 256], P('row', None, 'col')
- energy: float32 [], replicated
Inputs may be any that keep to these rules, and one draw needn't show every extreme that they name: `left_sector`: left sector s belongs to row s // 4. Block k belongs to row k // 8. The 8 blocks of one row name distinct left sectors; they name either none or exactly 2 sectors belonging to any one row, and the blocks of every row name 2 sectors belonging to one common row. `left_env`: each tile is symmetric in its last two dimensions. `right_env`: each tile is symmetric in its last two dimensions.
All inputs are finite; a program needn't handle non-finite values. No bound on the sum of `term_on` on one device may be relied on, other than what follows from the above.
Results may differ from a plain program's by a relative error of at most 0.0001.
Values sent between devices are 32-bit elements; how exact they have to be, the bound alone decides.
No kernel may reach another device: no remote copies, remote signals or barrier semaphores. Data moves between devices by JAX's collectives and lax.ppermute only.
A program may use at most 128 MiB of HBM per device.

v0:
```python
import jax
import jax.numpy as jnp
from jax import lax
from jax.sharding import PartitionSpec as P

ITERS = 2
highest = lax.Precision.HIGHEST


def lookup(small_table, index_list):
    slot_hits = index_list[:, None] == jnp.arange(small_table.shape[0], dtype=jnp.int32)[None, :]
    return jnp.sum(jnp.where(slot_hits, small_table[None, :], 0), axis=1)


def tile_masks(left_ids, right_ids, left_size, right_size, tile_size, offset, span_cols):
    rows_live = lookup(left_size, left_ids)
    cols_live = lookup(right_size, right_ids)
    row_mask = (jnp.arange(tile_size, dtype=jnp.int32)[None, :] < rows_live[:, None]).astype(
        jnp.float32
    )
    col_mask = (
        (offset + jnp.arange(span_cols, dtype=jnp.int32))[None, :] < cols_live[:, None]
    ).astype(jnp.float32)
    return row_mask[:, :, None] * col_mask[:, None, :]


def local(theta, left_env, right_env, left_sector, right_sector, term_on, left_size, right_size):
    row_count = lax.axis_size("row")
    blocks, tile_size, thin_cols = theta.shape
    local_sectors = left_env.shape[0]
    capacity = max(2, 2 * blocks // row_count)
    row_index = lax.axis_index("row")
    col_index = lax.axis_index("col")
    own_left = lax.dynamic_slice_in_dim(left_sector, row_index * blocks, blocks)
    offset = col_index * thin_cols
    span_cols = theta.shape[2]
    start_mask = tile_masks(
        own_left, right_sector, left_size, right_size, tile_size, offset, span_cols
    )
    start_vec = theta * start_mask
    senders = row_index * local_sectors + jnp.arange(local_sectors, dtype=jnp.int32)
    wanted = left_sector.reshape(row_count, blocks)
    used_flag = jnp.any(wanted[:, :, None] == senders[None, None, :], axis=1)
    used_count = used_flag.astype(jnp.int32)
    before = jnp.cumsum(used_count, axis=1) - used_count
    pick_flag = used_flag[:, None, :] & (
        before[:, None, :] == jnp.arange(capacity, dtype=jnp.int32)[None, :, None]
    )
    filled = jnp.any(pick_flag, axis=2).reshape(-1)
    local_index = jnp.sum(
        jnp.where(pick_flag, jnp.arange(local_sectors, dtype=jnp.int32)[None, None, :], 0), axis=2
    ).reshape(-1)
    outgoing = (
        jnp.take(left_env, local_index, axis=0) * filled.astype(jnp.float32)[:, None, None, None]
    )
    arrived = lax.all_to_all(outgoing, "row", split_axis=0, concat_axis=0, tiled=True)
    every_sector = jnp.arange(row_count * local_sectors, dtype=jnp.int32)
    needed = (
        jnp.any(own_left[:, None] == every_sector[None, :], axis=0)
        .astype(jnp.int32)
        .reshape(row_count, local_sectors)
    )
    order_rank = (jnp.cumsum(needed, axis=1) - needed).reshape(-1)
    position = own_left // local_sectors * capacity + lookup(order_rank, own_left)
    left_pick = jnp.take(arrived, position, axis=0)
    right_pick = jnp.take(right_env, right_sector, axis=0)
    weights = term_on.astype(jnp.float32)

    def contract(full_vector):
        middle = (
            jnp.einsum("swia,sab->swib", left_pick, full_vector, precision=highest)
            * weights[:, :, None, None]
        )
        return jnp.einsum("swib,swjb->sij", middle, right_pick, precision=highest)

    def operate(vector):
        full_vector = lax.all_gather(vector, "col", axis=2, tiled=True)
        total_sum = lax.psum_scatter(contract(full_vector), "col", scatter_dimension=2, tiled=True)
        return total_sum * start_mask

    def combine(values):
        reduced = lax.psum(values, ("row", "col"))
        return reduced

    image_vec = operate(start_vec)
    norm_sq, correlation = combine((jnp.sum(start_vec * start_vec), jnp.sum(start_vec * image_vec)))
    inv_norm = 1.0 / jnp.sqrt(norm_sq)
    basis_vec = start_vec * inv_norm
    applied = image_vec * inv_norm
    ritz_value = correlation / norm_sq
    for turn_index in range(ITERS):
        residual = applied - ritz_value * basis_vec
        (res_sq,) = combine((jnp.sum(residual * residual),))
        length = jnp.sqrt(res_sq)
        fresh_vec = residual / length
        fresh_applied = operate(fresh_vec)
        (curvature,) = combine((jnp.sum(fresh_vec * fresh_applied),))
        half_gap = 0.5 * (ritz_value - curvature)
        root_term = jnp.sqrt(half_gap * half_gap + res_sq)
        lowest = 0.5 * (ritz_value + curvature) - root_term
        first_coef = curvature - lowest
        pair_norm = jnp.sqrt(first_coef * first_coef + res_sq)
        basis_vec = (first_coef * basis_vec - length * fresh_vec) / pair_norm
        applied = (first_coef * applied - length * fresh_applied) / pair_norm
        ritz_value = lowest
    total_entries = blocks * row_count * tile_size * tile_size
    output = basis_vec * jnp.sqrt(jnp.float32(total_entries))
    return (output, ritz_value)


def solution(mesh):
    placed = (
        P("row", None, "col"),
        P("row", "col", None, None),
        P(None, "col", None, None),
        P(),
        P("row"),
        P("row", "col"),
        P(),
        P(),
    )
    return jax.shard_map(
        local, mesh=mesh, in_specs=placed, out_specs=(P("row", None, "col"), P()), check_vma=False
    )
```

profile of v0, /device:TPU:1, one launch (start us, length us, event | category | flops | bytes accessed | tf_op | source)
XLA Modules:
  0.0 820.7 jit_solution(7117098073512323360)
XLA Ops:
  7.2 0.9 eq.29
  8.9 4.3 gather_fusion
  13.2 7.9 select_multiply_fusion
  21.1 6.4 all-to-all-start
  28.6 0.7 multiply_multiply_fusion.3
  29.5 4.9 gather_fusion.2
  34.5 86.8 %all-to-all-done = f32[16,2,256,256]{3,2,1,0:T(8,128)} async-done(((f32[16,2,256,256]{3,2,1,0:T(8,128)}), f32[16,2,256,256]{3,2,1,0:T(8,128)}, u32[]{:S(2)}, u32[]{:S(2)}) %all-to-all-start) | async-done | bytes 8388640 | tf_op jit(solution)/shard_map/all_to_all | solution.py:56
  121.4 6.2 gather_fusion.1
  127.6 6.8 fusion.13
  134.4 5.9 fusion.33
  140.3 73.6 %reduce-scatter.4.cloned.1.call-done = f32[8,256,16]{1,2,0:T(8,128)} async-done(((f32[8,256,256]{1,2,0:T(8,128)}), f32[8,256,16]{1,2,0:T(8,128)}) %reduce-scatter.4.cloned.1.call-update) | async-done | bytes 131088 | tf_op jit(solution)/shard_map/reduce_scatter | solution.py:78
  213.9 1.6 multiply_reduce_fusion.4
  215.6 65.9 %all-reduce = (f32[]{:T(128)}, f32[]{:T(128)}) all-reduce(f32[]{:T(128)} %get-tuple-element.3, f32[]{:T(128)} %get-tuple-element.2), channel_id=1, replica_groups=mesh['row'=8,'col'=16] {'row','col'}, use_global_device_ids=true, to_apply=%region_13.14 | all-reduce | flops 2 | bytes 16 | tf_op jit(solution)/shard_map/psum | solution.py:82
  283.5 1.6 multiply_reduce_fusion.2
  285.1 62.7 %psum.44 = f32[]{:T(128)} all-reduce(f32[]{:T(128)} %multiply_reduce_fusion.2), channel_id=1, replica_groups=mesh['row'=8,'col'=16] {'row','col'}, use_global_device_ids=true, to_apply=%region_15.16 | all-reduce | flops 1 | bytes 8 | tf_op jit(solution)/shard_map/psum | solution.py:82
  348.5 1.7 broadcast_divide_fusion.1
  350.2 41.4 %all-gather.6.cloned.1.call-done = f32[8,256,256]{1,2,0:T(8,128)} async-done(((f32[8,256,16]{1,2,0:T(8,128)}), f32[8,256,256]{1,2,0:T(8,128)}) %all-gather.6.cloned.1.call-update) | async-done | bytes 2097168 | tf_op jit(solution)/shard_map/all_gather | solution.py:77
  391.6 6.8 fusion.11
  398.5 5.9 fusion.38
  404.4 73.2 %reduce-scatter.6.cloned.1.call-done = f32[8,256,16]{1,2,0:T(8,128)} async-done(((f32[8,256,256]{1,2,0:T(8,128)}), f32[8,256,16]{1,2,0:T(8,128)}) %reduce-scatter.6.cloned.1.call-update) | async-done | bytes 131088 | tf_op jit(solution)/shard_map/reduce_scatter | solution.py:78
  477.6 1.6 multiply_reduce_fusion.1
  479.2 65.8 %psum.45 = f32[]{:T(128)} all-reduce(f32[]{:T(128)} %multiply_reduce_fusion.1), channel_id=1, replica_groups=mesh['row'=8,'col'=16] {'row','col'}, use_global_device_ids=true, to_apply=%region_18.19 | all-reduce | flops 1 | bytes 8 | tf_op jit(solution)/shard_map/psum | solution.py:82
  548.3 1.7 multiply_reduce_fusion
  550.0 62.5 %psum.46 = f32[]{:T(128)} all-reduce(f32[]{:T(128)} %get-tuple-element.8), channel_id=1, replica_groups=mesh['row'=8,'col'=16] {'row','col'}, use_global_device_ids=true, to_apply=%region_20.21 | all-reduce | flops 1 | bytes 8 | tf_op jit(solution)/shard_map/psum | solution.py:82
  613.2 0.7 broadcast_divide_fusion
  614.2 41.2 %all-gather.8.cloned.1.call-done = f32[8,256,256]{1,2,0:T(8,128)} async-done(((f32[8,256,16]{1,2,0:T(8,128)}), f32[8,256,256]{1,2,0:T(8,128)}) %all-gather.8.cloned.1.call-update) | async-done | bytes 2097168 | tf_op jit(solution)/shard_map/all_gather | solution.py:77
  655.3 6.8 fusion.9
  662.1 5.9 fusion.43
  668.0 73.2 %reduce-scatter.8.cloned.1.call-done = f32[8,256,16]{1,2,0:T(8,128)} async-done(((f32[8,256,256]{1,2,0:T(8,128)}), f32[8,256,16]{1,2,0:T(8,128)}) %reduce-scatter.8.cloned.1.call-update) | async-done | bytes 131088 | tf_op jit(solution)/shard_map/reduce_scatter | solution.py:78
  741.3 1.6 fusion.49
  742.9 65.8 %psum.47 = f32[]{:T(128)} all-reduce(f32[]{:T(128)} %fusion.49), channel_id=1, replica_groups=mesh['row'=8,'col'=16] {'row','col'}, use_global_device_ids=true, to_apply=%region_23.24 | all-reduce | flops 1 | bytes 8 | tf_op jit(solution)/shard_map/psum | solution.py:82
  812.0 0.8 divide_multiply_fusion
  (72 shorter events, 2.5 us)
Async XLA Ops:
  7.2 1.7 copy-start
  21.1 6.4 copy-start.7
  21.1 6.9 copy-start.10
  21.1 7.0 copy-start.11
  21.1 7.1 copy-start.9
  21.1 7.5 copy-start.4
  21.1 8.3 %copy-start.8 = (s32[8,2]{0,1:T(2,128)S(1)}, s32[8,2]{0,1:T(2,128)}, u32[]{:S(2)}) copy-start(s32[8,2]{0,1:T(2,128)} %param.13) | copy-start | bytes 196
  21.1 100.3 %all-to-all-start = ((f32[16,2,256,256]{3,2,1,0:T(8,128)}), f32[16,2,256,256]{3,2,1,0:T(8,128)}, u32[]{:S(2)}, u32[]{:S(2)}) async-start(f32[16,2,256,256]{3,2,1,0:T(8,128)} %select_multiply_fusion), calls=%async_computation | async-start | bytes 16777216 | tf_op jit(solution)/shard_map/all_to_all | solution.py:56
  27.5 100.0 %all-gather.4.cloned.1.call-start = ((), (), s32[]{:S(2)}) async-start(), calls=%async_computation.4 | async-start | bytes 2228224 | tf_op jit(solution)/shard_map/all_gather | solution.py:77
  29.3 184.6 %reduce-scatter.4.cloned.1.call-start = ((), (), s32[]{:S(2)}) async-start(), calls=%async_computation.5 | async-start | bytes 2228224 | tf_op jit(solution)/shard_map/reduce_scatter | solution.py:78
  127.6 6.8 copy-start.1
  140.3 251.4 %all-gather.6.cloned.1.call-start = ((), (), s32[]{:S(2)}) async-start(), calls=%async_computation.6 | async-start | bytes 2228224 | tf_op jit(solution)/shard_map/all_gather | solution.py:77
  350.2 127.4 %reduce-scatter.6.cloned.1.call-start = ((), (), s32[]{:S(2)}) async-start(), calls=%async_computation.7 | async-start | bytes 2228224 | tf_op jit(solution)/shard_map/reduce_scatter | solution.py:78
  391.6 6.8 copy-start.2
  398.4 79.2 %copy-start.5 = (f32[8,256,16]{1,2,0:T(8,128)S(1)}, f32[8,256,16]{1,2,0:T(8,128)}, u32[]{:S(2)}) copy-start(f32[8,256,16]{1,2,0:T(8,128)} %broadcast_divide_fusion.1) | copy-start | bytes 393220
  398.4 149.9 %copy-start.6 = (f32[8,256,16]{1,2,0:T(8,128)S(1)}, f32[8,256,16]{1,2,0:T(8,128)}, u32[]{:S(2)}) copy-start(f32[8,256,16]{1,2,0:T(8,128)} %reduce-scatter.4.cloned.1.call-done) | copy-start | bytes 393220
  404.4 251.0 %all-gather.8.cloned.1.call-start = ((), (), s32[]{:S(2)}) async-start(), calls=%async_computation.8 | async-start | bytes 2228224 | tf_op jit(solution)/shard_map/all_gather | solution.py:77
  613.9 127.4 %reduce-scatter.8.cloned.1.call-start = ((), (), s32[]{:S(2)}) async-start(), calls=%async_computation.9 | async-start | bytes 2228224 | tf_op jit(solution)/shard_map/reduce_scatter | solution.py:78
  655.3 6.8 copy-start.3
Sparse Core Ops, SparseCore 0:
  31.1 46.3 all-gather.3
  140.4 73.5 reduce-scatter.3
  350.3 41.2 all-gather.5
  404.5 73.0 reduce-scatter.5
  614.0 41.2 all-gather.7
  668.2 73.0 reduce-scatter.7
where the time goes:
time: 822 us; the launch traced here: 821 us
  waiting for transfers between devices  390 us (47%)
  blocking collectives  323 us (39%)
  matrix products  38 us (5%)
  between operations  25.5 us (3%)
  other arithmetic  21.1 us (3%)
  local copies, waits for them, and re-layouts  17.1 us (2%)
    psum x5, blocking collectives, combine(): reduced = lax.psum(values, ('row', 'col'))  323 us
    reduce_scatter x3, waiting for transfers between devices, operate(): lax.psum_scatter(contract(full_vector), 'col', scatter_dimension=2, tiled...  220 us
    all_to_all x1, waiting for transfers between devices, local(): lax.all_to_all(outgoing, 'row', split_axis=0, concat_axis=0, tiled=True)  86.8 us
    all_gather x3, waiting for transfers between devices, operate(): full_vector = lax.all_gather(vector, 'col', axis=2, tiled=True)  82.6 us
    dot_general x3, matrix products, contract(): jnp.einsum('swia,sab->swib', left_pick, full_vector, precision=highest)  20.3 us
    dot_general x3, matrix products, contract(): return jnp.einsum('swib,swjb->sij', middle, right_pick, precision=highest)  17.6 us
  transfers between devices with their start and end apart: 7, of which 6 were waited for; matrix products, arithmetic and copies ran while one was open for 2% of the time, Pallas kernels for 0%

commit v1 on v0

--- a/solution.py
+++ b/solution.py
@@ -79,7 +79,12 @@
         return total_sum * start_mask
 
     def combine(values):
-        reduced = lax.psum(values, ("row", "col"))
+
+        def cut_files(piece_in):
+            now = lax.psum(lax.psum(piece_in, "row"), "col")
+            return now
+
+        reduced = cut_files(values)
         return reduced
 
     image_vec = operate(start_vec)

time: 822 us -> 755 us (0.918)
  blocking collectives: 323 us -> 239 us
  waiting for transfers between devices: 390 us -> 400 us
    psum x5 -> x10, blocking collectives: 323 us -> 239 us  [cut_files(): now = lax.psum(lax.psum(piece_in, 'row'), 'col')]
    all_gather x3, waiting for transfers between devices: 82.6 us -> 92.6 us  [operate(): full_vector = lax.all_gather(vector, 'col', axis=2, tiled=True)]
where the time goes in v1:
time: 755 us; the launch traced here: 747 us
  waiting for transfers between devices  400 us (53%)
  blocking collectives  239 us (32%)
  matrix products  38 us (5%)
  between operations  25.5 us (3%)
  other arithmetic  21.1 us (3%)
  local copies, waits for them, and re-layouts  17.1 us (2%)
    psum x10, blocking collectives, cut_files(): now = lax.psum(lax.psum(piece_in, 'row'), 'col')  239 us
    reduce_scatter x3, waiting for transfers between devices, operate(): lax.psum_scatter(contract(full_vector), 'col', scatter_dimension=2, tiled...  220 us
    all_gather x3, waiting for transfers between devices, operate(): full_vector = lax.all_gather(vector, 'col', axis=2, tiled=True)  92.6 us
    all_to_all x1, waiting for transfers between devices, local(): lax.all_to_all(outgoing, 'row', split_axis=0, concat_axis=0, tiled=True)  86.8 us
    dot_general x3, matrix products, contract(): jnp.einsum('swia,sab->swib', left_pick, full_vector, precision=highest)  20.3 us
    dot_general x3, matrix products, contract(): return jnp.einsum('swib,swjb->sij', middle, right_pick, precision=highest)  17.6 us
  transfers between devices with their start and end apart: 7, of which 6 were waited for; matrix products, arithmetic and copies ran while one was open for 2% of the time, Pallas kernels for 0%

profile of v1, /device:TPU:1, one launch (start us, length us, event | category | flops | bytes accessed | tf_op | source)
XLA Modules:
  0.0 747.1 jit_solution(459190305804180143)
XLA Ops:
  8.9 4.3 gather_fusion
  13.2 7.9 %select_multiply_fusion = f32[16,2,256,256]{3,2,1,0:T(8,128)} fusion(f32[16,2,256,256]{3,2,1,0:T(8,128)} %gather_fusion, f32[16]{0:T(128)S(1)} %reshape.149, pred[16]{0:T(512)(128)(4,1)S(1)} %compare_and_fusion.1), kind=kLoop, calls=%fused_computation.3 | loop fusion | flops 4194304 | bytes 16777296 | tf_op jit(solution)/shard_map/mul | solution.py:54
  21.1 6.4 all-to-all-start
  29.5 4.9 gather_fusion.2
  34.5 86.8 %all-to-all-done = f32[16,2,256,256]{3,2,1,0:T(8,128)} async-done(((f32[16,2,256,256]{3,2,1,0:T(8,128)}), f32[16,2,256,256]{3,2,1,0:T(8,128)}, u32[]{:S(2)}, u32[]{:S(2)}) %all-to-all-start) | async-done | bytes 8388640 | tf_op jit(solution)/shard_map/all_to_all | solution.py:56
  121.4 6.2 gather_fusion.1
  127.6 6.8 fusion.13
  134.4 5.9 fusion.33
  140.3 73.6 %reduce-scatter.4.cloned.1.call-done = f32[8,256,16]{1,2,0:T(8,128)} async-done(((f32[8,256,256]{1,2,0:T(8,128)}), f32[8,256,16]{1,2,0:T(8,128)}) %reduce-scatter.4.cloned.1.call-update) | async-done | bytes 131088 | tf_op jit(solution)/shard_map/reduce_scatter | solution.py:78
  213.9 1.6 multiply_reduce_fusion.4
  215.6 14.7 %all-reduce.1 = (f32[]{:T(128)}, f32[]{:T(128)}) all-reduce(f32[]{:T(128)} %get-tuple-element.3, f32[]{:T(128)} %get-tuple-element.2), channel_id=1, replica_groups=mesh['row'=8,'col'=16] {'row'}, use_global_device_ids=true, to_apply=%region_14.15 | all-reduce | flops 2 | bytes 16 | tf_op jit(solution)/shard_map/psum | solution.py:84
  230.3 31.8 %all-reduce = (f32[]{:T(128)}, f32[]{:T(128)}) all-reduce(f32[]{:T(128)} %get-tuple-element.8, f32[]{:T(128)} %get-tuple-element.9), channel_id=1, replica_groups=mesh['row'=8,'col'=16] {'col'}, use_global_device_ids=true, to_apply=%region_15.16 | all-reduce | flops 2 | bytes 16 | tf_op jit(solution)/shard_map/psum | solution.py:84
  264.1 1.6 multiply_reduce_fusion.2
  265.7 20.5 %psum.88 = f32[]{:T(128)} all-reduce(f32[]{:T(128)} %multiply_reduce_fusion.2), channel_id=1, replica_groups=mesh['row'=8,'col'=16] {'row'}, use_global_device_ids=true, to_apply=%region_17.18 | all-reduce | flops 1 | bytes 8 | tf_op jit(solution)/shard_map/psum | solution.py:84
  286.2 29.1 %psum.89 = f32[]{:T(128)} all-reduce(f32[]{:T(128)} %psum.88), channel_id=1, replica_groups=mesh['row'=8,'col'=16] {'col'}, use_global_device_ids=true, to_apply=%region_18.19 | all-reduce | flops 1 | bytes 8 | tf_op jit(solution)/shard_map/psum | solution.py:84
  316.0 1.7 broadcast_divide_fusion.1
  318.0 46.3 %all-gather.6.cloned.1.call-done = f32[8,256,256]{1,2,0:T(8,128)} async-done(((f32[8,256,16]{1,2,0:T(8,128)}), f32[8,256,256]{1,2,0:T(8,128)}) %all-gather.6.cloned.1.call-update) | async-done | bytes 2097168 | tf_op jit(solution)/shard_map/all_gather | solution.py:77
  364.3 6.8 fusion.11
  371.1 5.9 fusion.38
  377.1 73.2 %reduce-scatter.6.cloned.1.call-done = f32[8,256,16]{1,2,0:T(8,128)} async-done(((f32[8,256,256]{1,2,0:T(8,128)}), f32[8,256,16]{1,2,0:T(8,128)}) %reduce-scatter.6.cloned.1.call-update) | async-done | bytes 131088 | tf_op jit(solution)/shard_map/reduce_scatter | solution.py:78
  450.2 1.6 multiply_reduce_fusion.1
  451.9 14.7 %psum.90 = f32[]{:T(128)} all-reduce(f32[]{:T(128)} %multiply_reduce_fusion.1), channel_id=1, replica_groups=mesh['row'=8,'col'=16] {'row'}, use_global_device_ids=true, to_apply=%region_21.22 | all-reduce | flops 1 | bytes 8 | tf_op jit(solution)/shard_map/psum | solution.py:84
  466.5 31.8 %psum.91 = f32[]{:T(128)} all-reduce(f32[]{:T(128)} %psum.90), channel_id=1, replica_groups=mesh['row'=8,'col'=16] {'col'}, use_global_device_ids=true, to_apply=%region_22.23 | all-reduce | flops 1 | bytes 8 | tf_op jit(solution)/shard_map/psum | solution.py:84
  501.7 1.7 multiply_reduce_fusion
  503.4 20.5 %psum.92 = f32[]{:T(128)} all-reduce(f32[]{:T(128)} %get-tuple-element.10), channel_id=1, replica_groups=mesh['row'=8,'col'=16] {'row'}, use_global_device_ids=true, to_apply=%region_24.25 | all-reduce | flops 1 | bytes 8 | tf_op jit(solution)/shard_map/psum | solution.py:84
  523.9 29.2 %psum.93 = f32[]{:T(128)} all-reduce(f32[]{:T(128)} %psum.92), channel_id=1, replica_groups=mesh['row'=8,'col'=16] {'col'}, use_global_device_ids=true, to_apply=%region_25.26 | all-reduce | flops 1 | bytes 8 | tf_op jit(solution)/shard_map/psum | solution.py:84
  554.7 46.3 %all-gather.8.cloned.1.call-done = f32[8,256,256]{1,2,0:T(8,128)} async-done(((f32[8,256,16]{1,2,0:T(8,128)}), f32[8,256,256]{1,2,0:T(8,128)}) %all-gather.8.cloned.1.call-update) | async-done | bytes 2097168 | tf_op jit(solution)/shard_map/all_gather | solution.py:77
  601.0 6.8 fusion.9
  607.8 5.9 fusion.43
  613.7 73.2 %reduce-scatter.8.cloned.1.call-done = f32[8,256,16]{1,2,0:T(8,128)} async-done(((f32[8,256,256]{1,2,0:T(8,128)}), f32[8,256,16]{1,2,0:T(8,128)}) %reduce-scatter.8.cloned.1.call-update) | async-done | bytes 131088 | tf_op jit(solution)/shard_map/reduce_scatter | solution.py:78
  688.5 14.7 %psum.94 = f32[]{:T(128)} all-reduce(f32[]{:T(128)} %fusion.49), channel_id=1, replica_groups=mesh['row'=8,'col'=16] {'row'}, use_global_device_ids=true, to_apply=%region_28.29 | all-reduce | flops 1 | bytes 8 | tf_op jit(solution)/shard_map/psum | solution.py:84
  703.2 31.8 %psum.95 = f32[]{:T(128)} all-reduce(f32[]{:T(128)} %psum.94), channel_id=1, replica_groups=mesh['row'=8,'col'=16] {'col'}, use_global_device_ids=true, to_apply=%region_29.30 | all-reduce | flops 1 | bytes 8 | tf_op jit(solution)/shard_map/psum | solution.py:84
  (77 shorter events, 7.4 us)
Async XLA Ops:
  7.2 1.7 copy-start
  21.1 6.4 copy-start.7
  21.1 6.9 copy-start.10
  21.1 7.0 copy-start.11
  21.1 7.1 copy-start.9
  21.1 7.5 %copy-start.4 = (f32[8,256,16]{1,2,0:T(8,128)S(1)}, f32[8,256,16]{1,2,0:T(8,128)}, u32[]{:S(2)}) copy-start(f32[8,256,16]{1,2,0:T(8,128)} %param.8) | copy-start | bytes 393220
  21.1 8.3 %copy-start.8 = (s32[8,2]{0,1:T(2,128)S(1)}, s32[8,2]{0,1:T(2,128)}, u32[]{:S(2)}) copy-start(s32[8,2]{0,1:T(2,128)} %param.13) | copy-start | bytes 196
  21.1 100.3 %all-to-all-start = ((f32[16,2,256,256]{3,2,1,0:T(8,128)}), f32[16,2,256,256]{3,2,1,0:T(8,128)}, u32[]{:S(2)}, u32[]{:S(2)}) async-start(f32[16,2,256,256]{3,2,1,0:T(8,128)} %select_multiply_fusion), calls=%async_computation | async-start | bytes 16777216 | tf_op jit(solution)/shard_map/all_to_all | solution.py:56
  27.5 100.0 %all-gather.4.cloned.1.call-start = ((), (), s32[]{:S(2)}) async-start(), calls=%async_computation.4 | async-start | bytes 2228224 | tf_op jit(solution)/shard_map/all_gather | solution.py:77
  29.3 184.6 %reduce-scatter.4.cloned.1.call-start = ((), (), s32[]{:S(2)}) async-start(), calls=%async_computation.5 | async-start | bytes 2228224 | tf_op jit(solution)/shard_map/reduce_scatter | solution.py:78
  127.6 6.8 copy-start.1
  140.3 224.0 %all-gather.6.cloned.1.call-start = ((), (), s32[]{:S(2)}) async-start(), calls=%async_computation.6 | async-start | bytes 2228224 | tf_op jit(solution)/shard_map/all_gather | solution.py:77
  317.7 132.5 %reduce-scatter.6.cloned.1.call-start = ((), (), s32[]{:S(2)}) async-start(), calls=%async_computation.7 | async-start | bytes 2228224 | tf_op jit(solution)/shard_map/reduce_scatter | solution.py:78
  364.3 6.8 copy-start.2
  371.1 79.2 %copy-start.5 = (f32[8,256,16]{1,2,0:T(8,128)S(1)}, f32[8,256,16]{1,2,0:T(8,128)}, u32[]{:S(2)}) copy-start(f32[8,256,16]{1,2,0:T(8,128)} %broadcast_divide_fusion.1) | copy-start | bytes 393220
  371.1 130.6 %copy-start.6 = (f32[8,256,16]{1,2,0:T(8,128)S(1)}, f32[8,256,16]{1,2,0:T(8,128)}, u32[]{:S(2)}) copy-start(f32[8,256,16]{1,2,0:T(8,128)} %reduce-scatter.4.cloned.1.call-done) | copy-start | bytes 393220
  377.0 224.0 %all-gather.8.cloned.1.call-start = ((), (), s32[]{:S(2)}) async-start(), calls=%async_computation.8 | async-start | bytes 2228224 | tf_op jit(solution)/shard_map/all_gather | solution.py:77
  554.4 132.5 %reduce-scatter.8.cloned.1.call-start = ((), (), s32[]{:S(2)}) async-start(), calls=%async_computation.9 | async-start | bytes 2228224 | tf_op jit(solution)/shard_map/reduce_scatter | solution.py:78
  601.0 6.8 copy-start.3
Sparse Core Ops, SparseCore 0:
  31.1 46.3 all-gather.3
  140.4 73.5 reduce-scatter.3
  317.9 46.3 all-gather.5
  377.1 73.0 reduce-scatter.5
  554.6 46.3 all-gather.7
  613.8 73.0 reduce-scatter.7
